TPU v7x, 32 devices: a whole 2x2x4 slice. The times are simulated.
32 devices in a mesh: batch: 4 (over y, x), corpus: 8 (over z, core).
Axes of the slice: x: 2, y: 2, z: 4, core: 2. Of those that a mesh axis runs over, the one named last changes fastest.
Arguments:
- states: bfloat16 [4096, 4096], P('batch', 'corpus'), may hold values from -6 to 6
- norm_gain: float32 [4096], replicated, may hold values from 0.25 to 1.75
- gate_weight: bfloat16 [4096, 12288], P('batch', 'corpus'), may hold values from -0.09375 to 0.09375
- up_weight: bfloat16 [4096, 12288], P('batch', 'corpus'), may hold values from -0.09375 to 0.09375
- down_weight: bfloat16 [12288, 4096], P('corpus', 'batch'), may hold values from -0.0546875 to 0.0546875
- final_gain: float32 [4096], replicated, may hold values from 0.25 to 1.75
- hash_weight: bfloat16 [4096, 1024], replicated, may hold values from -0.75 to 0.75
- query_bits: bfloat16 [4096, 1024], replicated, may hold values from -1 to 1
- slot_map: int32 [64], replicated, may hold values from 0 to 63, each once
- query_index: int32 [4096, 100], replicated, may hold values from 0 to 63
Outputs:
- scores: float32 [4096, 100], P(('batch', 'corpus'))
Inputs may be any that keep to these rules, and one draw needn't show every extreme that they name: `slot_map`: each corpus entry is named by exactly one document.
All inputs are finite; a program needn't handle non-finite values.
Results may differ from a plain program's by a relative error of at most 0.017.
Values may be sent and summed in bfloat16 or wider, within the bound.
A program may use at most 192 MiB of HBM per device.

v0:
```python
import jax
import jax.numpy as jnp
from jax import lax
from jax.sharding import PartitionSpec as P

DOC_LEN = 64
CODE = 1024
NQ = 4096


def rms(values, gain):
    return values * lax.rsqrt(jnp.mean(values * values, axis=-1, keepdims=True) + 1e-06) * gain


def add_rows(left, piece):
    return jnp.dot(left, piece, preferred_element_type=jnp.float32)


def local(
    states,
    norm_gain,
    gate_weight,
    up_weight,
    down_weight,
    final_gain,
    hash_weight,
    query_bits,
    slot_map,
    query_index,
):
    corpus_count = lax.axis_size("corpus")
    devices = lax.axis_size("batch") * corpus_count
    flat_index = lax.axis_index("batch") * corpus_count + lax.axis_index("corpus")
    whole = lax.all_gather(states, "corpus", axis=1, tiled=True)
    normed = rms(whole.astype(jnp.float32), norm_gain).astype(jnp.bfloat16)

    def add_one(piece):
        return add_rows(normed, piece)

    gate = add_one(lax.all_gather(gate_weight, "batch", axis=0, tiled=True))
    up = add_one(lax.all_gather(up_weight, "batch", axis=0, tiled=True))
    hidden = (jax.nn.silu(gate) * up).astype(jnp.bfloat16)
    terms = jnp.dot(
        hidden,
        lax.all_gather(down_weight, "batch", axis=1, tiled=True),
        preferred_element_type=jnp.float32,
    )
    ffn = lax.psum_scatter(
        terms.astype(jnp.bfloat16), "corpus", scatter_dimension=0, tiled=True
    ).astype(jnp.float32)
    own_rows = ffn.shape[0]
    mine = lax.dynamic_slice_in_dim(whole, lax.axis_index("corpus") * own_rows, own_rows, 0)
    resid = mine.astype(jnp.float32) + ffn
    finals = rms(resid, final_gain)
    owned_docs = own_rows // DOC_LEN
    pooled = jnp.mean(finals.reshape(owned_docs, DOC_LEN, finals.shape[1]), axis=1).astype(
        jnp.bfloat16
    )
    codes = jnp.tanh(jnp.dot(pooled, hash_weight, preferred_element_type=jnp.float32)).astype(
        jnp.bfloat16
    )
    doc_total = owned_docs * devices
    scale = 1.0 / jnp.sqrt(jnp.float32(CODE))
    gathered = lax.all_gather(codes, ("batch", "corpus"), axis=0, tiled=True)
    placing = (slot_map[:, None] == jnp.arange(doc_total, dtype=jnp.int32)[None, :]).astype(
        jnp.bfloat16
    )
    corpus = jnp.einsum("ds,dc->sc", placing, gathered, preferred_element_type=jnp.float32).astype(
        jnp.bfloat16
    )
    query_rows = NQ // devices
    my_bits = lax.dynamic_slice_in_dim(query_bits, flat_index * query_rows, query_rows, 0)
    my_index = lax.dynamic_slice_in_dim(query_index, flat_index * query_rows, query_rows, 0)
    table = jnp.dot(my_bits, corpus.T, preferred_element_type=jnp.float32) * scale
    scores = jnp.take_along_axis(table, my_index, axis=1)
    return scores


def solution(mesh):
    placed = (
        P("batch", "corpus"),
        P(),
        P("batch", "corpus"),
        P("batch", "corpus"),
        P("corpus", "batch"),
        P(),
        P(),
        P(),
        P(),
        P(),
    )
    return jax.shard_map(
        local, mesh=mesh, in_specs=placed, out_specs=P(("batch", "corpus"), None), check_vma=False
    )
```

profile of v0, /device:TPU:0, one launch (start us, length us, event | category | flops | bytes accessed | tf_op | source)
XLA Modules:
  0.0 712.4 jit_solution(285428027022941697)
XLA Ops:
  6.5 0.0 copy-start
  6.5 0.0 all-gather.6.cloned.1.call-start
  6.5 0.7 all-gather.6.cloned.1.call-update
  7.3 0.0 copy-start.3
  7.3 0.0 all-gather.8.cloned.1.call-start
  7.3 0.7 all-gather.8.cloned.1.call-update
  8.0 0.0 all-gather.10.cloned.1.call-start
  8.1 0.7 all-gather.10.cloned.1.call-update
  8.8 0.0 all-gather.12.cloned.1.call-start
  8.8 0.5 all-gather.12.cloned.1.call-update
  9.3 0.0 reduce-scatter.2.cloned.1.call-start
  9.4 84.4 %all-gather.6.cloned.1.call-done = bf16[1024,4096]{1,0:T(8,128)(2,1)} async-done(((bf16[1024,512]{1,0:T(8,128)(2,1)}), bf16[1024,4096]{1,0:T(8,128)(2,1)}) %all-gather.6.cloned.1.call-update) | async-done | bytes 8388624 | tf_op jit(solution)/shard_map/all_gather | solution.py:34
  93.7 5.1 fusion
  98.8 117.7 %all-gather.8.cloned.1.call-done = bf16[4096,1536]{1,0:T(8,128)(2,1)} async-done(((bf16[1024,1536]{1,0:T(8,128)(2,1)}), bf16[4096,1536]{1,0:T(8,128)(2,1)}) %all-gather.8.cloned.1.call-update) | async-done | bytes 12582928 | tf_op jit(solution)/shard_map/all_gather | solution.py:40
  216.5 0.0 copy-done.3
  216.5 19.7 %fusion.4 = f32[1024,1536]{1,0:T(8,128)} fusion(bf16[4096,1536]{1,0:T(8,128)(2,1)} %all-gather.8.cloned.1.call-done, bf16[1024,4096]{1,0:T(8,128)(2,1)} %all-gather.6.cloned.1.call-done, f32[4096]{0:T(1024)S(1)} %copy-done.3, f32[1024]{0:T(1024)S(1)} %add_rsqrt_fusion), kind=kOutput, calls=%fused_computation.8 | convolution fusion | flops 12901679104 | bytes 27283456 | tf_op jit(solution)/shard_map/dot_general | solution.py:16
  236.2 104.6 %all-gather.10.cloned.1.call-done = bf16[4096,1536]{1,0:T(8,128)(2,1)} async-done(((bf16[1024,1536]{1,0:T(8,128)(2,1)}), bf16[4096,1536]{1,0:T(8,128)(2,1)}) %all-gather.10.cloned.1.call-update) | async-done | bytes 12582928 | tf_op jit(solution)/shard_map/all_gather | solution.py:41
  340.7 20.6 %multiply_convert_fusion = bf16[1024,1536]{1,0:T(8,128)(2,1)} fusion(f32[1024,1536]{1,0:T(8,128)} %fusion.4, bf16[4096,1536]{1,0:T(8,128)(2,1)} %all-gather.10.cloned.1.call-done, bf16[1024,4096]{1,0:T(8,128)(2,1)} %all-gather.6.cloned.1.call-done, f32[4096]{0:T(1024)S(1)} %copy-done.3, f32[1024]{0:T(1024)S(1)} %add_rsqrt_fusion), kind=kOutput, calls=%fused_computation.7 | convolution fusion | flops 12911116288 | bytes 30429184 | tf_op jit(solution)/shard_map/dot_general | solution.py:16
  361.4 103.5 %all-gather.12.cloned.1.call-done = bf16[1536,4096]{1,0:T(8,128)(2,1)} async-done(((bf16[1536,1024]{1,0:T(8,128)(2,1)}), bf16[1536,4096]{1,0:T(8,128)(2,1)}) %all-gather.12.cloned.1.call-update) | async-done | bytes 12582928 | tf_op jit(solution)/shard_map/all_gather | solution.py:45
  464.9 19.1 %convolution_convert_fusion = bf16[1024,4096]{1,0:T(8,128)(2,1)} fusion(bf16[1024,1536]{1,0:T(8,128)(2,1)} %multiply_convert_fusion, bf16[1536,4096]{1,0:T(8,128)(2,1)} %all-gather.12.cloned.1.call-done), kind=kOutput, calls=%fused_computation.6 | convolution fusion | flops 12889096192 | bytes 24117248 | tf_op jit(solution)/shard_map/dot_general | solution.py:43
  483.9 0.0 copy-start.1
  483.9 0.0 reduce-scatter.2.cloned.1.call-update
  483.9 0.0 copy-done
  484.0 0.1 copy.15
  484.1 0.1 reshape.33
  484.2 89.4 %reduce-scatter.2.cloned.1.call-done = bf16[128,4096]{1,0:T(8,128)(2,1)} async-done(((bf16[1024,4096]{1,0:T(8,128)(2,1)}), bf16[128,4096]{1,0:T(8,128)(2,1)}) %reduce-scatter.2.cloned.1.call-update) | async-done | bytes 1048592 | tf_op jit(solution)/shard_map/reduce_scatter | solution.py:48
  573.6 2.0 multiply_reduce_fusion
  575.6 0.0 copy-done.1
  575.6 2.0 bitcast_reduce_fusion
  577.6 0.0 copy-start.2
  577.7 4.6 fusion.9
  582.2 39.5 %all-gather = bf16[32,2,1024]{2,1,0:T(2,128)(2,1)S(1)} all-gather(bf16[1,2,1024]{2,1,0:T(2,128)(2,1)S(1)} %fusion.9), channel_id=1, replica_groups=mesh['batch'=4,'corpus'=8] {'batch','corpus'}, dimensions={0}, use_global_device_ids=true | all-gather | bytes 135168 | tf_op jit(solution)/shard_map/all_gather | solution.py:64
  621.7 0.1 reshape.45
  621.8 0.0 copy-done.2
  621.8 1.4 fusion.7
  623.2 81.8 %gather_fusion = f32[12800]{0:T(1024)S(1)} fusion(f32[128,64]{0,1:T(8,128)S(1)} %fusion.7, s32[12800]{0:T(1024)S(1)} %reshape.33), kind=kCustom, calls=%fused_computation | custom fusion | bytes 204800 | tf_op jit(solution)/shard_map/jit(take_along_axis)/gather | solution.py:75
  705.0 0.1 reshape.36
  705.2 0.7 copy.14
  (5 shorter events, 0.1 us)
Async XLA Ops:
  6.5 477.4 %copy-start = (s32[4096,100]{0,1:T(8,128)S(1)}, s32[4096,100]{0,1:T(8,128)}, u32[]{:S(2)}) copy-start(s32[4096,100]{0,1:T(8,128)} %param.19) | copy-start | bytes 4915204
  6.5 87.2 %all-gather.6.cloned.1.call-start = ((), (), s32[]{:S(2)}) async-start(), calls=%async_computation.1 | async-start | bytes 9437184 | tf_op jit(solution)/shard_map/all_gather | solution.py:34
  7.3 209.2 %copy-start.3 = (f32[4096]{0:T(1024)S(1)}, f32[4096]{0:T(1024)}, u32[]{:S(2)}) copy-start(f32[4096]{0:T(1024)} %param.11) | copy-start | bytes 49156
  7.3 209.2 %all-gather.8.cloned.1.call-start = ((), (), s32[]{:S(2)}) async-start(), calls=%async_computation.2 | async-start | bytes 15728640 | tf_op jit(solution)/shard_map/all_gather | solution.py:40
  8.0 332.7 %all-gather.10.cloned.1.call-start = ((), (), s32[]{:S(2)}) async-start(), calls=%async_computation.3 | async-start | bytes 15728640 | tf_op jit(solution)/shard_map/all_gather | solution.py:41
  8.8 456.1 %all-gather.12.cloned.1.call-start = ((), (), s32[]{:S(2)}) async-start(), calls=%async_computation.4 | async-start | bytes 15728640 | tf_op jit(solution)/shard_map/all_gather | solution.py:45
  9.3 564.3 %reduce-scatter.2.cloned.1.call-start = ((), (), s32[]{:S(2)}) async-start(), calls=%async_computation.5 | async-start | bytes 9437184 | tf_op jit(solution)/shard_map/reduce_scatter | solution.py:48
  483.9 91.7 %copy-start.1 = (f32[4096]{0:T(1024)S(1)}, f32[4096]{0:T(1024)}, u32[]{:S(2)}) copy-start(f32[4096]{0:T(1024)} %param.15) | copy-start | bytes 49156
  577.6 44.1 %copy-start.2 = (s32[64]{0:T(128)S(1)}, s32[64]{0:T(128)}, u32[]{:S(2)}) copy-start(s32[64]{0:T(128)} %param.18) | copy-start | bytes 772
Sparse Core Ops, SparseCore 0:
  8.9 84.7 all-gather.5
  95.6 120.8 all-gather.7
  218.3 122.3 all-gather.9
  342.4 122.3 all-gather.11
  484.1 89.5 reduce-scatter.1
where the time goes:
time: 713 us; the launch traced here: 712 us
  waiting for transfers between devices  502 us (70%)
  local copies, waits for them, and re-layouts  82.9 us (12%)
  matrix products  65.3 us (9%)
  blocking collectives  39.5 us (6%)
  between operations  13.3 us (2%)
  other arithmetic  9.15 us (1%)
    all_gather x1, waiting for transfers between devices, local(): gate = add_one(lax.all_gather(gate_weight, 'batch', axis=0, tiled=True))  118 us
    all_gather x1, waiting for transfers between devices, local(): up = add_one(lax.all_gather(up_weight, 'batch', axis=0, tiled=True))  105 us
    all_gather x1, waiting for transfers between devices, local(): lax.all_gather(down_weight, 'batch', axis=1, tiled=True)  103 us
    reduce_scatter x1, waiting for transfers between devices, local(): lax.psum_scatter(terms.astype(jnp.bfloat16), 'corpus', scatter_dimension=...  89.4 us
    all_gather x1, waiting for transfers between devices, local(): whole = lax.all_gather(states, 'corpus', axis=1, tiled=True)  84.4 us
    gather x3, local copies, waits for them, and re-layouts, local(): scores = jnp.take_along_axis(table, my_index, axis=1)  82 us
    dot_general x2, matrix products, add_rows(): return jnp.dot(left, piece, preferred_element_type=jnp.float32)  40.3 us
    all_gather x1, blocking collectives, local(): gathered = lax.all_gather(codes, ('batch', 'corpus'), axis=0, tiled=True)  39.5 us
  transfers between devices with their start and end apart: 5, of which 5 were waited for; matrix products, arithmetic and copies ran while one was open for 6% of the time, Pallas kernels for 0%

commit v1 on v0

--- a/solution.py
+++ b/solution.py
@@ -1,6 +1,8 @@
 import jax
 import jax.numpy as jnp
 from jax import lax
+from jax.experimental import pallas as pl
+from jax.experimental.pallas import tpu as pltpu
 from jax.sharding import PartitionSpec as P
 
 DOC_LEN = 64
@@ -14,6 +16,27 @@
 
 def add_rows(left, piece):
     return jnp.dot(left, piece, preferred_element_type=jnp.float32)
+
+
+def score_kernel(bits_ref, corpus_ref, index_ref, out_ref):
+    table = lax.dot_general(
+        bits_ref[...],
+        corpus_ref[...],
+        (((1,), (1,)), ((), ())),
+        preferred_element_type=jnp.float32,
+    ) * (1.0 / float(bits_ref.shape[1]) ** 0.5)
+    out_ref[...] = jnp.take_along_axis(table, index_ref[...], axis=1)
+
+
+def score(bits, corpus, index):
+    rows, top = index.shape
+    lanes = 128 * max(pl.cdiv(corpus.shape[0], 128), pl.cdiv(top, 128))
+    corpus = jnp.pad(corpus, ((0, lanes - corpus.shape[0]), (0, 0)))
+    index = jnp.pad(index, ((0, 0), (0, lanes - top)))
+    wide = pl.pallas_call(
+        score_kernel, out_shape=jax.ShapeDtypeStruct((rows, lanes), jnp.float32)
+    )(bits, corpus, index)
+    return wide[:, :top]
 
 
 def local(
@@ -60,7 +83,6 @@
         jnp.bfloat16
     )
     doc_total = owned_docs * devices
-    scale = 1.0 / jnp.sqrt(jnp.float32(CODE))
     gathered = lax.all_gather(codes, ("batch", "corpus"), axis=0, tiled=True)
     placing = (slot_map[:, None] == jnp.arange(doc_total, dtype=jnp.int32)[None, :]).astype(
         jnp.bfloat16
@@ -71,9 +93,7 @@
     query_rows = NQ // devices
     my_bits = lax.dynamic_slice_in_dim(query_bits, flat_index * query_rows, query_rows, 0)
     my_index = lax.dynamic_slice_in_dim(query_index, flat_index * query_rows, query_rows, 0)
-    table = jnp.dot(my_bits, corpus.T, preferred_element_type=jnp.float32) * scale
-    scores = jnp.take_along_axis(table, my_index, axis=1)
-    return scores
+    return score(my_bits, corpus, my_index)
 
 
 def solution(mesh):

time: 713 us -> 633 us (0.89)
  local copies, waits for them, and re-layouts: 82.9 us -> 4.75 us
    gather x3 -> x0, local copies, waits for them, and re-layouts: 82 us -> none  [local(): scores = jnp.take_along_axis(table, my_index, axis=1)]
  transfers between devices with their start and end apart: 5 -> 5, of which waited for: 5 -> 5; matrix products, arithmetic and copies ran while one was open for 6% -> 8% of each run, Pallas kernels for 0% -> 0%
where the time goes in v1:
time: 633 us
  waiting for transfers between devices  500 us (79%)
  matrix products  64.2 us (10%)
  blocking collectives  39.5 us (6%)
  between operations  13.2 us (2%)
  other arithmetic  9.1 us (1%)
    all_gather x1, waiting for transfers between devices, local(): gate = add_one(lax.all_gather(gate_weight, 'batch', axis=0, tiled=True))  118 us
    all_gather x1, waiting for transfers between devices, local(): up = add_one(lax.all_gather(up_weight, 'batch', axis=0, tiled=True))  105 us
    all_gather x1, waiting for transfers between devices, local(): lax.all_gather(down_weight, 'batch', axis=1, tiled=True)  103 us
    reduce_scatter x1, waiting for transfers between devices, local(): lax.psum_scatter(terms.astype(jnp.bfloat16), 'corpus', scatter_dimension=...  87.2 us
    all_gather x1, waiting for transfers between devices, local(): whole = lax.all_gather(states, 'corpus', axis=1, tiled=True)  84.4 us
    dot_general x2, matrix products, add_rows(): return jnp.dot(left, piece, preferred_element_type=jnp.float32)  40.3 us
    all_gather x1, blocking collectives, local(): gathered = lax.all_gather(codes, ('batch', 'corpus'), axis=0, tiled=True)  39.5 us
    dot_general x1, matrix products, local(): jnp.dot(hidden, lax.all_gather(down_weight, 'batch', axis=1, tiled=True),...  19.1 us
  transfers between devices with their start and end apart: 5, of which 5 were waited for; matrix products, arithmetic and copies ran while one was open for 8% of the time, Pallas kernels for 0%

profile of v1, /device:TPU:0, one launch (start us, length us, event | category | flops | bytes accessed | tf_op | source)
XLA Modules:
  0.0 632.9 jit_solution(12196887923452314875)
XLA Ops:
  6.5 0.0 copy-start
  6.5 0.0 all-gather.6.cloned.1.call-start
  6.5 0.7 all-gather.6.cloned.1.call-update
  7.3 0.0 copy-start.3
  7.3 0.0 all-gather.8.cloned.1.call-start
  7.3 0.7 all-gather.8.cloned.1.call-update
  8.0 0.0 all-gather.10.cloned.1.call-start
  8.1 0.7 all-gather.10.cloned.1.call-update
  8.8 0.0 all-gather.12.cloned.1.call-start
  8.8 0.5 all-gather.12.cloned.1.call-update
  9.3 0.0 reduce-scatter.2.cloned.1.call-start
  9.4 84.4 %all-gather.6.cloned.1.call-done = bf16[1024,4096]{1,0:T(8,128)(2,1)} async-done(((bf16[1024,512]{1,0:T(8,128)(2,1)}), bf16[1024,4096]{1,0:T(8,128)(2,1)}) %all-gather.6.cloned.1.call-update) | async-done | bytes 8388624 | tf_op jit(solution)/shard_map/all_gather | solution.py:57
  93.7 5.1 fusion
  98.8 117.7 %all-gather.8.cloned.1.call-done = bf16[4096,1536]{1,0:T(8,128)(2,1)} async-done(((bf16[1024,1536]{1,0:T(8,128)(2,1)}), bf16[4096,1536]{1,0:T(8,128)(2,1)}) %all-gather.8.cloned.1.call-update) | async-done | bytes 12582928 | tf_op jit(solution)/shard_map/all_gather | solution.py:63
  216.5 0.0 copy-done.3
  216.5 19.7 %fusion.4 = f32[1024,1536]{1,0:T(8,128)} fusion(bf16[4096,1536]{1,0:T(8,128)(2,1)} %all-gather.8.cloned.1.call-done, bf16[1024,4096]{1,0:T(8,128)(2,1)} %all-gather.6.cloned.1.call-done, f32[4096]{0:T(1024)S(1)} %copy-done.3, f32[1024]{0:T(1024)S(1)} %add_rsqrt_fusion), kind=kOutput, calls=%fused_computation.7 | convolution fusion | flops 12901679104 | bytes 27283456 | tf_op jit(solution)/shard_map/dot_general | solution.py:18
  236.2 104.6 %all-gather.10.cloned.1.call-done = bf16[4096,1536]{1,0:T(8,128)(2,1)} async-done(((bf16[1024,1536]{1,0:T(8,128)(2,1)}), bf16[4096,1536]{1,0:T(8,128)(2,1)}) %all-gather.10.cloned.1.call-update) | async-done | bytes 12582928 | tf_op jit(solution)/shard_map/all_gather | solution.py:64
  340.7 20.6 %multiply_convert_fusion = bf16[1024,1536]{1,0:T(8,128)(2,1)} fusion(f32[1024,1536]{1,0:T(8,128)} %fusion.4, bf16[4096,1536]{1,0:T(8,128)(2,1)} %all-gather.10.cloned.1.call-done, bf16[1024,4096]{1,0:T(8,128)(2,1)} %all-gather.6.cloned.1.call-done, f32[4096]{0:T(1024)S(1)} %copy-done.3, f32[1024]{0:T(1024)S(1)} %add_rsqrt_fusion), kind=kOutput, calls=%fused_computation.6 | convolution fusion | flops 12911116288 | bytes 30429184 | tf_op jit(solution)/shard_map/dot_general | solution.py:18
  361.4 103.5 %all-gather.12.cloned.1.call-done = bf16[1536,4096]{1,0:T(8,128)(2,1)} async-done(((bf16[1536,1024]{1,0:T(8,128)(2,1)}), bf16[1536,4096]{1,0:T(8,128)(2,1)}) %all-gather.12.cloned.1.call-update) | async-done | bytes 12582928 | tf_op jit(solution)/shard_map/all_gather | solution.py:68
  464.9 19.1 %convolution_convert_fusion = bf16[1024,4096]{1,0:T(8,128)(2,1)} fusion(bf16[1024,1536]{1,0:T(8,128)(2,1)} %multiply_convert_fusion, bf16[1536,4096]{1,0:T(8,128)(2,1)} %all-gather.12.cloned.1.call-done), kind=kOutput, calls=%fused_computation.5 | convolution fusion | flops 12889096192 | bytes 24117248 | tf_op jit(solution)/shard_map/dot_general | solution.py:66
  483.9 0.0 copy-start.1
  483.9 0.0 reduce-scatter.2.cloned.1.call-update
  483.9 0.0 copy-done
  484.0 0.1 copy.15
  484.1 0.6 pad.9.index_ref
  484.7 1.7 constant_dynamic-slice_fusion.1.bits_ref
  486.4 87.2 %reduce-scatter.2.cloned.1.call-done = bf16[128,4096]{1,0:T(8,128)(2,1)} async-done(((bf16[1024,4096]{1,0:T(8,128)(2,1)}), bf16[128,4096]{1,0:T(8,128)(2,1)}) %reduce-scatter.2.cloned.1.call-update) | async-done | bytes 1048592 | tf_op jit(solution)/shard_map/reduce_scatter | solution.py:71
  573.6 2.0 multiply_reduce_fusion
  575.6 0.0 copy-done.1
  575.6 2.0 bitcast_reduce_fusion
  577.6 0.0 copy-start.2
  577.7 4.6 fusion.7
  582.2 39.5 %all-gather = bf16[32,2,1024]{2,1,0:T(2,128)(2,1)S(1)} all-gather(bf16[1,2,1024]{2,1,0:T(2,128)(2,1)S(1)} %fusion.7), channel_id=1, replica_groups=mesh['batch'=4,'corpus'=8] {'batch','corpus'}, dimensions={0}, use_global_device_ids=true | all-gather | bytes 135168 | tf_op jit(solution)/shard_map/all_gather | solution.py:86
  621.7 0.1 reshape.24
  621.8 0.0 copy-done.2
  621.8 0.3 convolution_convert_fusion.1
  622.1 0.7 pad.8.corpus_ref
  622.8 2.0 shard_map.100
  624.8 1.6 copy.14
  (3 shorter events, 0.0 us)
Async XLA Ops:
  6.5 477.4 %copy-start = (s32[4096,100]{0,1:T(8,128)S(1)}, s32[4096,100]{0,1:T(8,128)}, u32[]{:S(2)}) copy-start(s32[4096,100]{0,1:T(8,128)} %param.19) | copy-start | bytes 4915204
  6.5 87.2 %all-gather.6.cloned.1.call-start = ((), (), s32[]{:S(2)}) async-start(), calls=%async_computation.1 | async-start | bytes 9437184 | tf_op jit(solution)/shard_map/all_gather | solution.py:57
  7.3 209.2 %copy-start.3 = (f32[4096]{0:T(1024)S(1)}, f32[4096]{0:T(1024)}, u32[]{:S(2)}) copy-start(f32[4096]{0:T(1024)} %param.11) | copy-start | bytes 49156
  7.3 209.2 %all-gather.8.cloned.1.call-start = ((), (), s32[]{:S(2)}) async-start(), calls=%async_computation.2 | async-start | bytes 15728640 | tf_op jit(solution)/shard_map/all_gather | solution.py:63
  8.0 332.7 %all-gather.10.cloned.1.call-start = ((), (), s32[]{:S(2)}) async-start(), calls=%async_computation.3 | async-start | bytes 15728640 | tf_op jit(solution)/shard_map/all_gather | solution.py:64
  8.8 456.1 %all-gather.12.cloned.1.call-start = ((), (), s32[]{:S(2)}) async-start(), calls=%async_computation.4 | async-start | bytes 15728640 | tf_op jit(solution)/shard_map/all_gather | solution.py:68
  9.3 564.3 %reduce-scatter.2.cloned.1.call-start = ((), (), s32[]{:S(2)}) async-start(), calls=%async_computation.5 | async-start | bytes 9437184 | tf_op jit(solution)/shard_map/reduce_scatter | solution.py:71
  483.9 91.7 %copy-start.1 = (f32[4096]{0:T(1024)S(1)}, f32[4096]{0:T(1024)}, u32[]{:S(2)}) copy-start(f32[4096]{0:T(1024)} %param.15) | copy-start | bytes 49156
  577.6 44.1 %copy-start.2 = (s32[64]{0:T(128)S(1)}, s32[64]{0:T(128)}, u32[]{:S(2)}) copy-start(s32[64]{0:T(128)} %param.18) | copy-start | bytes 772
Sparse Core Ops, SparseCore 0:
  8.9 84.7 all-gather.5
  95.6 120.8 all-gather.7
  218.3 122.3 all-gather.9
  342.4 122.3 all-gather.11
  484.1 89.5 reduce-scatter.1

commit v2 on v1

--- a/solution.py
+++ b/solution.py
@@ -37,6 +37,480 @@
         score_kernel, out_shape=jax.ShapeDtypeStruct((rows, lanes), jnp.float32)
     )(bits, corpus, index)
     return wide[:, :top]
+
+
+def wide_kernel(
+    states_ref, gain_ref, gate_ref, up_ref, down_ref, out_ref,
+    X, G, U, W, N, H, SR, YR, ZR,
+    s_loc, s_y, s_zr, s_zl, s_sib, w_loc, w_x, w_y, w_r, c_sib, c_y, c_z,
+):
+    nz = lax.axis_size("corpus") // 2
+    b = lax.axis_index("batch")
+    c = lax.axis_index("corpus")
+    y, x = b // 2, b % 2
+    z, k = c // 2, c % 2
+    rows, feat = states_ref.shape
+    half = W.shape[0]
+    full = X.shape[1]
+    cols = down_ref.shape[1]
+    w = cols // 2
+    by, bx, bd = (1 - y) * 2 + x, y * 2 + (1 - x), (1 - y) * 2 + (1 - x)
+    to_y = {"batch": by}
+    to_x = {"batch": bx}
+    to_sib = {"corpus": z * 2 + (1 - k)}
+
+    def at_z(other):
+        return {"corpus": other * 2 + k}
+
+    def remote(src, dst, sems, place):
+        return pltpu.make_async_remote_copy(
+            src_ref=src, dst_ref=dst, send_sem=sems.at[0], recv_sem=sems.at[1],
+            device_id=place, device_id_type=pl.DeviceIdType.MESH,
+        )
+
+    def spot(t, zs, ks):
+        block = y if t == 0 else 1 - y
+        return X.at[
+            pl.ds(pl.multiple_of(block * rows, rows), rows),
+            pl.ds(pl.multiple_of((zs * 2 + ks) * feat, feat), feat),
+        ]
+
+    own_states = pltpu.make_async_copy(states_ref, spot(0, z, k), s_loc)
+    y_states = remote(states_ref, X.at[
+        pl.ds(pl.multiple_of(y * rows, rows), rows),
+        pl.ds(pl.multiple_of(c * feat, feat), feat),
+    ], s_y, to_y)
+
+    def right(t, s):
+        src = states_ref if t == 0 and s == 0 else spot(t, z - s, k)
+        return remote(src, spot(t, z - s, k), s_zr.at[t, s], at_z(z + 1))
+
+    def left(t, s):
+        src = states_ref if t == 0 and s == 0 else spot(t, z + s, k)
+        return remote(src, spot(t, z + s, k), s_zl.at[t, s], at_z(z - 1))
+
+    def sib(t, zs):
+        return remote(spot(t, zs, k), spot(t, zs, k), s_sib.at[t, zs], to_sib)
+
+    def sib_in(t, zs):
+        return remote(spot(t, zs, 1 - k), spot(t, zs, 1 - k), s_sib.at[t, zs], to_sib)
+
+    def first(t):
+        @pl.when(z + 1 < nz)
+        def _():
+            right(t, 0).start()
+
+        @pl.when(z >= 1)
+        def _():
+            left(t, 0).start()
+
+        sib(t, z).start()
+
+    def relay(t, s):
+        @pl.when(z - 1 - s >= 0)
+        def _():
+            right(t, s).wait_recv()
+            if s + 1 < nz - 1:
+                @pl.when(z + 1 < nz)
+                def _():
+                    right(t, s + 1).start()
+            sib(t, z - 1 - s).start()
+
+        @pl.when(z + 1 + s < nz)
+        def _():
+            left(t, s).wait_recv()
+            if s + 1 < nz - 1:
+                @pl.when(z >= 1)
+                def _():
+                    left(t, s + 1).start()
+            sib(t, z + 1 + s).start()
+
+    def part(m, mine):
+        h = pl.ds(pl.multiple_of((y if mine else 1 - y) * half, half), half)
+        if m == 2:
+            return down_ref.at[h, :]
+        return (gate_ref, up_ref)[m].at[:, h]
+
+    def place(m, block):
+        if m == 2:
+            return W.at[:, pl.ds(pl.multiple_of(block * cols, cols), cols)]
+        return (G, U)[m].at[pl.ds(pl.multiple_of(block * rows_w, rows_w), rows_w), :]
+
+    rows_w = gate_ref.shape[0]
+    loc = [pltpu.make_async_copy(part(m, True), place(m, b), w_loc.at[m]) for m in range(3)]
+    wx = [remote(part(m, True), place(m, b), w_x.at[m], to_x) for m in range(3)]
+    wy = [remote(part(m, False), place(m, b), w_y.at[m], to_y) for m in range(3)]
+    wr = [remote(place(m, by), place(m, by), w_r.at[m], to_x) for m in range(3)]
+
+    y_states.start()
+    own_states.start()
+    wx[0].start()
+    for m in range(3):
+        wy[m].start()
+    wx[1].start()
+    own_states.wait()
+    first(0)
+    for m in range(3):
+        loc[m].start()
+    y_states.wait_recv()
+    first(1)
+    for s in range(nz - 1):
+        relay(0, s)
+        if s == nz - 2:
+            wy[0].wait_recv()
+            wr[0].start()
+    for s in range(nz - 1):
+        relay(1, s)
+        if s == 0:
+            wy[1].wait_recv()
+            wr[1].start()
+            wx[2].start()
+    wy[2].wait_recv()
+    wr[2].start()
+    for m in range(3):
+        loc[m].wait()
+    for t in range(2):
+        for zs in range(nz):
+            sib_in(t, zs).wait_recv()
+    for m in range(2):
+        wx[m].wait_recv()
+        wr[m].wait_recv()
+    y_states.wait_send()
+    for t in range(2):
+        for zs in range(nz):
+            sib(t, zs).wait_send()
+        for s in range(nz - 1):
+            @pl.when((z - s >= 0) & (z + 1 < nz))
+            def _():
+                right(t, s).wait_send()
+
+            @pl.when((z + s < nz) & (z >= 1))
+            def _():
+                left(t, s).wait_send()
+
+    tile = N.shape[0]
+    gain = gain_ref[...]
+
+    @pl.loop(0, X.shape[0] // tile)
+    def _(i):
+        r = pl.ds(pl.multiple_of(i * tile, tile), tile)
+
+        @pl.loop(0, tile // 32)
+        def _(p):
+            q = pl.multiple_of(p * 32, 32)
+            v = X[pl.ds(pl.multiple_of(i * tile + q, 32), 32), :].astype(jnp.float32)
+            scale = lax.rsqrt(jnp.mean(v * v, axis=-1, keepdims=True) + 1e-06)
+            N[pl.ds(q, 32), :] = (v * scale * gain).astype(jnp.bfloat16)
+
+        step = half // 3 if (half // 3) % 128 == 0 else 128
+
+        @pl.loop(0, half // step)
+        def _(j):
+            h = pl.ds(pl.multiple_of(j * step, 128), step)
+            g = jnp.dot(N[...], G[:, h], preferred_element_type=jnp.float32)
+            u = jnp.dot(N[...], U[:, h], preferred_element_type=jnp.float32)
+            H[r, h] = (g * jax.nn.sigmoid(g) * u).astype(jnp.bfloat16)
+
+    blocks = [x, 2 + x, 1 - x, 2 + (1 - x)]
+    own_rows = out_ref.shape[0]
+    for j in range(4):
+        out_ref[:, pl.ds(pl.multiple_of(blocks[j] * w, w), w)] = X[
+            pl.ds(pl.multiple_of(y * rows + z * own_rows, own_rows), own_rows),
+            pl.ds(pl.multiple_of(blocks[j] * cols + k * w, w), w),
+        ].astype(jnp.float32)
+
+    base = full // 2
+
+    def down_cols(j, core):
+        return pl.ds(pl.multiple_of(blocks[j] * cols + core * w, w), w)
+
+    def sib_sum(j):
+        return remote(X.at[:, pl.ds(j * w, w)], SR.at[j], c_sib.at[j], to_sib)
+
+    def y_sum(j):
+        return remote(X.at[pl.ds(0, rows), pl.ds(base + j * w, w)], YR.at[j], c_y.at[j], to_y)
+
+    def z_sum(j, dz):
+        to = lax.rem(z + dz, nz)
+        return remote(
+            X.at[
+                pl.ds(pl.multiple_of(rows + to * own_rows, own_rows), own_rows),
+                pl.ds(base + j * w, w),
+            ],
+            ZR.at[j, dz - 1], c_z.at[j, dz - 1], at_z(to),
+        )
+
+    piece = min(512, rows)
+
+    def step_a(j):
+        @pl.loop(0, 2 * rows // piece)
+        def _(i):
+            r = pl.ds(pl.multiple_of(i * piece, piece), piece)
+            X[r, pl.ds(j * w, w)] = jnp.dot(
+                H[r, :], W[:, down_cols(j, 1 - k)], preferred_element_type=jnp.float32
+            ).astype(jnp.bfloat16)
+
+        sib_sum(j).start()
+
+    def step_b(j):
+        sib_sum(j).wait_recv()
+        for put, block in ((0, 1 - y), (1, y)):
+            @pl.loop(0, rows // piece)
+            def _(i):
+                r = pl.ds(pl.multiple_of(block * rows + i * piece, piece), piece)
+                X[pl.ds(pl.multiple_of(put * rows + i * piece, piece), piece), pl.ds(base + j * w, w)] = (
+                    jnp.dot(H[r, :], W[:, down_cols(j, k)], preferred_element_type=jnp.float32)
+                    + SR[j, r, :].astype(jnp.float32)
+                ).astype(jnp.bfloat16)
+
+            if put == 0:
+                y_sum(j).start()
+
+    def step_c(j):
+        y_sum(j).wait_recv()
+
+        @pl.loop(0, rows // own_rows)
+        def _(i):
+            r = pl.ds(pl.multiple_of(rows + i * own_rows, own_rows), own_rows)
+            here = pl.ds(base + j * w, w)
+            X[r, here] = (
+                X[r, here].astype(jnp.float32)
+                + YR[j, pl.ds(pl.multiple_of(i * own_rows, own_rows), own_rows), :].astype(jnp.float32)
+            ).astype(jnp.bfloat16)
+
+        for dz in range(1, nz):
+            z_sum(j, dz).start()
+
+    def step_e(j):
+        here = pl.ds(pl.multiple_of(blocks[j] * w, w), w)
+        total = out_ref[:, here] + X[
+            pl.ds(pl.multiple_of(rows + z * own_rows, own_rows), own_rows), pl.ds(base + j * w, w)
+        ].astype(jnp.float32)
+        for dz in range(1, nz):
+            z_sum(j, dz).wait_recv()
+            total = total + ZR[j, dz - 1].astype(jnp.float32)
+        out_ref[:, here] = total
+
+    step_a(0)
+    step_a(1)
+    step_b(0)
+    step_b(1)
+    wx[2].wait_recv()
+    wr[2].wait_recv()
+    step_a(2)
+    step_c(0)
+    step_a(3)
+    step_b(2)
+    step_c(1)
+    step_b(3)
+    step_e(0)
+    step_c(2)
+    step_e(1)
+    step_c(3)
+    step_e(2)
+    step_e(3)
+    for j in range(4):
+        sib_sum(j).wait_send()
+        y_sum(j).wait_send()
+        for dz in range(1, nz):
+            z_sum(j, dz).wait_send()
+    for m in range(3):
+        wx[m].wait_send()
+        wy[m].wait_send()
+        wr[m].wait_send()
+
+
+def wide(states, norm_gain, gate_weight, up_weight, down_weight):
+    nz = lax.axis_size("corpus") // 2
+    rows, feat = states.shape
+    full = norm_gain.shape[0]
+    half = gate_weight.shape[1] // 2
+    cols = down_weight.shape[1]
+    w = cols // 2
+    own_rows = rows // nz
+    dma = pltpu.SemaphoreType.DMA
+    tile = min(512, rows)
+    any_spec = pl.BlockSpec(memory_space=pl.ANY)
+    vmem = pl.BlockSpec(memory_space=pltpu.VMEM)
+    return pl.pallas_call(
+        wide_kernel,
+        out_shape=jax.ShapeDtypeStruct((own_rows, full // 2), jnp.float32),
+        in_specs=[any_spec, vmem, any_spec, any_spec, any_spec],
+        out_specs=vmem,
+        scratch_shapes=[
+            pltpu.VMEM((2 * rows, full), jnp.bfloat16),
+            pltpu.VMEM((full, half), jnp.bfloat16),
+            pltpu.VMEM((full, half), jnp.bfloat16),
+            pltpu.VMEM((half, full), jnp.bfloat16),
+            pltpu.VMEM((tile, full), jnp.bfloat16),
+            pltpu.VMEM((2 * rows, half), jnp.bfloat16),
+            pltpu.VMEM((4, 2 * rows, w), jnp.bfloat16),
+            pltpu.VMEM((4, rows, w), jnp.bfloat16),
+            pltpu.VMEM((4, nz - 1, own_rows, w), jnp.bfloat16),
+            dma, dma((2,)), dma((2, nz - 1, 2)), dma((2, nz - 1, 2)), dma((2, nz, 2)),
+            dma((3,)), dma((3, 2)), dma((3, 2)), dma((3, 2)),
+            dma((4, 2)), dma((4, 2)), dma((4, nz - 1, 2)),
+        ],
+        compiler_params=pltpu.CompilerParams(
+            has_side_effects=True, vmem_limit_bytes=67043328
+        ),
+    )(states, norm_gain[None], gate_weight, up_weight, down_weight)
+
+
+def code_kernel(resid_ref, gain_ref, hash_ref, out_ref, HV, SQ, PB, CA, h_sem, q_sem, p_sem, a_send, a_recv):
+    corpus = lax.axis_size("corpus")
+    devices = lax.axis_size("batch") * corpus
+    b = lax.axis_index("batch")
+    c = lax.axis_index("corpus")
+    k = c % 2
+    me = b * corpus + c
+    to_sib = {"corpus": c + 1 - 2 * k}
+    own_rows, full_half = resid_ref.shape
+    w = HV.shape[1]
+    docs = own_rows // DOC_LEN
+    fetch = pltpu.make_async_copy(
+        hash_ref.at[:, pl.ds(pl.multiple_of(k * w, w), w)], HV, h_sem
+    )
+    fetch.start()
+
+    def swap(buf, sems):
+        return pltpu.make_async_remote_copy(
+            src_ref=buf.at[0], dst_ref=buf.at[1], send_sem=sems.at[0], recv_sem=sems.at[1],
+            device_id=to_sib, device_id_type=pl.DeviceIdType.MESH,
+        )
+
+    square = jnp.sum(resid_ref[...] * resid_ref[...], axis=1, keepdims=True)
+    SQ[0] = jnp.broadcast_to(square, SQ.shape[1:])
+    swap(SQ, q_sem).start()
+    swap(SQ, q_sem).wait()
+    scale = lax.rsqrt((square + SQ[1][:, :1]) / float(2 * full_half) + 1e-06)
+    final = resid_ref[...] * scale * gain_ref[...]
+    pooled = [
+        jnp.mean(final[d * DOC_LEN : (d + 1) * DOC_LEN], axis=0, keepdims=True)
+        for d in range(docs)
+    ]
+    pooled.append(jnp.zeros((PB.shape[1] - docs, full_half), jnp.float32))
+    PB[0] = jnp.concatenate(pooled, axis=0).astype(jnp.bfloat16)
+    swap(PB, p_sem).start()
+    fetch.wait()
+    swap(PB, p_sem).wait()
+    total = None
+    parts = lax.axis_size("batch")
+    span = full_half // parts
+    for n in range(parts):
+        for side in range(2):
+            core = k if side == 0 else 1 - k
+            term = jnp.dot(
+                PB[side, :, n * span : (n + 1) * span],
+                HV[pl.ds(pl.multiple_of(n * 2 * span + core * span, span), span), :],
+                preferred_element_type=jnp.float32,
+            )
+            total = term if total is None else total + term
+    codes = jnp.tanh(total)[:docs]
+    lanes = CA.shape[2]
+    CA[me] = jnp.concatenate(
+        [codes[:, q * lanes : (q + 1) * lanes] for q in range(w // lanes)], axis=0
+    ).astype(jnp.bfloat16)
+
+    def tell(step):
+        to = lax.rem(me + step, devices)
+        return pltpu.make_async_remote_copy(
+            src_ref=CA.at[me], dst_ref=CA.at[me],
+            send_sem=a_send.at[step - 1], recv_sem=a_recv.at[step - 1],
+            device_id={"batch": to // corpus, "corpus": to % corpus},
+            device_id_type=pl.DeviceIdType.MESH,
+        )
+
+    def heard(step):
+        src = lax.rem(me + devices - step, devices)
+        return pltpu.make_async_remote_copy(
+            src_ref=CA.at[src], dst_ref=CA.at[src],
+            send_sem=a_send.at[step - 1], recv_sem=a_recv.at[step - 1],
+            device_id={"batch": src // corpus, "corpus": src % corpus},
+            device_id_type=pl.DeviceIdType.MESH,
+        )
+
+    @pl.loop(1, devices)
+    def _(step):
+        tell(step).start()
+
+    @pl.loop(1, devices)
+    def _(step):
+        heard(step).wait_recv()
+
+    @pl.loop(1, devices)
+    def _(step):
+        tell(step).wait_send()
+
+    out_ref[...] = CA[...]
+
+
+def all_codes(resid, final_gain, hash_weight):
+    parts = lax.axis_size("batch")
+    corpus = lax.axis_size("corpus")
+    devices = parts * corpus
+    own_rows, full_half = resid.shape
+    docs = own_rows // DOC_LEN
+    bits = hash_weight.shape[1]
+    w = bits // 2
+    gain = lax.dynamic_index_in_dim(
+        final_gain.reshape(parts, 2, full_half // parts), lax.axis_index("corpus") % 2, 1, False
+    ).reshape(1, full_half)
+    vmem = pl.BlockSpec(memory_space=pltpu.VMEM)
+    dma = pltpu.SemaphoreType.DMA
+    groups = w // 128
+    got = pl.pallas_call(
+        code_kernel,
+        out_shape=jax.ShapeDtypeStruct((devices, groups * docs, 128), jnp.bfloat16),
+        in_specs=[vmem, vmem, pl.BlockSpec(memory_space=pl.ANY)],
+        out_specs=vmem,
+        scratch_shapes=[
+            pltpu.VMEM((2 * full_half, w), jnp.bfloat16),
+            pltpu.VMEM((2, own_rows, 128), jnp.float32),
+            pltpu.VMEM((2, 16, full_half), jnp.bfloat16),
+            pltpu.VMEM((devices, groups * docs, 128), jnp.bfloat16),
+            dma, dma((2,)), dma((2,)), dma((devices - 1,)), dma((devices - 1,)),
+        ],
+        compiler_params=pltpu.CompilerParams(
+            has_side_effects=True, vmem_limit_bytes=40 * 1024 * 1024
+        ),
+    )(resid, gain, hash_weight)
+    got = got.reshape(parts, corpus // 2, 2, groups, docs, 128)
+    return got.transpose(0, 1, 4, 2, 3, 5).reshape(devices // 2 * docs, bits)
+
+
+def plain_codes(
+    states, norm_gain, gate_weight, up_weight, down_weight, final_gain, hash_weight
+):
+    whole = lax.all_gather(states, "corpus", axis=1, tiled=True)
+    normed = rms(whole.astype(jnp.float32), norm_gain).astype(jnp.bfloat16)
+
+    def add_one(piece):
+        return add_rows(normed, piece)
+
+    gate = add_one(lax.all_gather(gate_weight, "batch", axis=0, tiled=True))
+    up = add_one(lax.all_gather(up_weight, "batch", axis=0, tiled=True))
+    hidden = (jax.nn.silu(gate) * up).astype(jnp.bfloat16)
+    terms = jnp.dot(
+        hidden,
+        lax.all_gather(down_weight, "batch", axis=1, tiled=True),
+        preferred_element_type=jnp.float32,
+    )
+    ffn = lax.psum_scatter(
+        terms.astype(jnp.bfloat16), "corpus", scatter_dimension=0, tiled=True
+    ).astype(jnp.float32)
+    own_rows = ffn.shape[0]
+    mine = lax.dynamic_slice_in_dim(whole, lax.axis_index("corpus") * own_rows, own_rows, 0)
+    resid = mine.astype(jnp.float32) + ffn
+    finals = rms(resid, final_gain)
+    owned_docs = own_rows // DOC_LEN
+    pooled = jnp.mean(finals.reshape(owned_docs, DOC_LEN, finals.shape[1]), axis=1).astype(
+        jnp.bfloat16
+    )
+    codes = jnp.tanh(jnp.dot(pooled, hash_weight, preferred_element_type=jnp.float32)).astype(
+        jnp.bfloat16
+    )
+    return lax.all_gather(codes, ("batch", "corpus"), axis=0, tiled=True)
 
 
 def local(
@@ -54,36 +528,12 @@
     corpus_count = lax.axis_size("corpus")
     devices = lax.axis_size("batch") * corpus_count
     flat_index = lax.axis_index("batch") * corpus_count + lax.axis_index("corpus")
-    whole = lax.all_gather(states, "corpus", axis=1, tiled=True)
-    normed = rms(whole.astype(jnp.float32), norm_gain).astype(jnp.bfloat16)
-
-    def add_one(piece):
-        return add_rows(normed, piece)
-
-    gate = add_one(lax.all_gather(gate_weight, "batch", axis=0, tiled=True))
-    up = add_one(lax.all_gather(up_weight, "batch", axis=0, tiled=True))
-    hidden = (jax.nn.silu(gate) * up).astype(jnp.bfloat16)
-    terms = jnp.dot(
-        hidden,
-        lax.all_gather(down_weight, "batch", axis=1, tiled=True),
-        preferred_element_type=jnp.float32,
-    )
-    ffn = lax.psum_scatter(
-        terms.astype(jnp.bfloat16), "corpus", scatter_dimension=0, tiled=True
-    ).astype(jnp.float32)
-    own_rows = ffn.shape[0]
-    mine = lax.dynamic_slice_in_dim(whole, lax.axis_index("corpus") * own_rows, own_rows, 0)
-    resid = mine.astype(jnp.float32) + ffn
-    finals = rms(resid, final_gain)
-    owned_docs = own_rows // DOC_LEN
-    pooled = jnp.mean(finals.reshape(owned_docs, DOC_LEN, finals.shape[1]), axis=1).astype(
-        jnp.bfloat16
-    )
-    codes = jnp.tanh(jnp.dot(pooled, hash_weight, preferred_element_type=jnp.float32)).astype(
-        jnp.bfloat16
-    )
-    doc_total = owned_docs * devices
-    gathered = lax.all_gather(codes, ("batch", "corpus"), axis=0, tiled=True)
+    layer = (states, norm_gain, gate_weight, up_weight, down_weight)
+    if lax.axis_size("batch") == 4 and corpus_count == 8:
+        gathered = all_codes(wide(*layer), final_gain, hash_weight)
+    else:
+        gathered = plain_codes(*layer, final_gain, hash_weight)
+    doc_total = gathered.shape[0]
     placing = (slot_map[:, None] == jnp.arange(doc_total, dtype=jnp.int32)[None, :]).astype(
         jnp.bfloat16
     )

time: 633 us -> 365 us (0.58)
  waiting for transfers between devices: 500 us -> 0 us
  Pallas kernels: 1.96 us -> 352 us
  matrix products: 64.2 us -> 0.29 us
  blocking collectives: 39.5 us -> 0 us
  between operations: 13.2 us -> 0.07 us
  other arithmetic: 9.1 us -> 0 us
  local copies, waits for them, and re-layouts: 4.75 us -> 12.6 us
    all_gather x4 -> x0, waiting for transfers between devices: 410 us -> none  [the longest x1 118 us: local(): gate = add_one(lax.all_gather(gate_weight, 'batch', axis=0, tiled=True))]
    pallas_call x0 -> x2, Pallas kernels: none -> 350 us  [the longest x1 333 us: wide(): pl.pallas_call(wide_kernel, out_shape=jax.ShapeDtypeStruct((own_rows, ful...]
    reduce_scatter x1 -> x0, waiting for transfers between devices: 87.2 us -> none  [local(): lax.psum_scatter(terms.astype(jnp.bfloat16), 'corpus', scatter_dimension=...]
    dot_general x4 -> x0, matrix products: 63.9 us -> none  [the longest x2 40.3 us: add_rows(): return jnp.dot(left, piece, preferred_element_type=jnp.float32)]
    all_gather x1 -> x0, blocking collectives: 39.5 us -> none  [local(): gathered = lax.all_gather(codes, ('batch', 'corpus'), axis=0, tiled=True)]
    reduce_sum x3 -> x0, other arithmetic: 9.08 us -> none  [the longest x2 7.03 us: rms(): jnp.mean(values * values, axis=-1, keepdims=True) + 1e-06]
  transfers between devices with their start and end apart: 5 -> 0, of which waited for: 5 -> 0; matrix products, arithmetic and copies ran while one was open for 8% -> 0% of each run, Pallas kernels for 0% -> 0%
where the time goes in v2:
time: 365 us
  Pallas kernels  352 us (96%)
  local copies, waits for them, and re-layouts  12.6 us (3%)
    pallas_call x1, Pallas kernels, wide(): pl.pallas_call(wide_kernel, out_shape=jax.ShapeDtypeStruct((own_rows, ful...  333 us
    pallas_call x1, Pallas kernels, all_codes(): pl.pallas_call(code_kernel, out_shape=jax.ShapeDtypeStruct((devices, grou...  17.3 us

profile of v2, /device:TPU:0, one launch (start us, length us, event | category | flops | bytes accessed | tf_op | source)
XLA Modules:
  0.0 364.8 jit_solution(435681839050524046)
XLA Ops:
  0.0 0.7 reshape.14
  0.7 0.6 constant_dynamic-slice_fusion.1
  1.3 332.6 %shard_map.100.resid_ref = f32[256,2048]{1,0:T(8,128)} custom-call(bf16[1024,512]{1,0:T(8,128)(2,1)} %states_ref.1, f32[1,4096]{1,0:T(1,128)} %bitcast.12, bf16[1024,1536]{1,0:T(8,128)(2,1)} %gate_ref.1, bf16[1024,1536]{1,0:T(8,128)(2,1)} %up_ref.1, bf16[1536,1024]{1,0:T(8,128)(2,1)} %down_ref.1), custom_call_target="tpu_custom_call" | custom-call | tf_op jit(solution)/shard_map/pallas_call | solution.py:335
  334.0 0.0 copy-start
  334.0 3.4 copy-done
  337.3 0.0 copy-start.1
  337.3 1.6 copy-done.1
  338.9 0.0 copy-start.2
  338.9 0.7 copy-done.2
  339.6 0.0 copy-start.3
  339.6 17.3 %shard_map.101 = bf16[32,16,128]{2,1,0:T(8,128)(2,1)S(1)} custom-call(f32[256,2048]{1,0:T(8,128)S(1)} %copy-done.1, f32[1,2048]{1,0:T(1,128)S(1)} %bitcast.9, bf16[4096,1024]{1,0:T(8,128)(2,1)S(1)} %copy-done), custom_call_target="tpu_custom_call" | custom-call | tf_op jit(solution)/shard_map/pallas_call | solution.py:462
  356.9 0.1 copy.18
  357.0 0.1 reshape.17
  357.1 0.0 copy-done.3
  357.1 0.3 convolution_convert_fusion
  357.4 0.7 pad.8.corpus_ref
  358.1 1.7 constant_dynamic-slice_fusion.2.bits_ref
  359.8 0.8 constant_dynamic-slice_fusion
  360.6 0.1 copy.16
  360.7 0.6 pad.9.index_ref
  361.3 2.0 shard_map.102
  363.3 1.6 copy.15
Async XLA Ops:
  334.0 3.4 copy-start
  337.3 1.6 copy-start.1
  338.9 0.7 copy-start.2
  339.6 17.5 %copy-start.3 = (s32[64]{0:T(128)S(1)}, s32[64]{0:T(128)}, u32[]{:S(2)}) copy-start(s32[64]{0:T(128)} %param.18) | copy-start | bytes 772

commit v3 on v2

--- a/solution.py
+++ b/solution.py
@@ -41,7 +41,7 @@
 
 def wide_kernel(
     states_ref, gain_ref, gate_ref, up_ref, down_ref, out_ref,
-    X, G, U, W, N, H, SR, YR, ZR,
+    X, G, U, W, AG, AU, H, SR, YR, ZR,
     s_loc, s_y, s_zr, s_zl, s_sib, w_loc, w_x, w_y, w_r, c_sib, c_y, c_z,
 ):
     nz = lax.axis_size("corpus") // 2
@@ -142,6 +142,70 @@
     wy = [remote(part(m, False), place(m, b), w_y.at[m], to_y) for m in range(3)]
     wr = [remote(place(m, by), place(m, by), w_r.at[m], to_x) for m in range(3)]
 
+    def settle(t):
+        for zs in range(nz):
+            sib_in(t, zs).wait_recv()
+            sib(t, zs).wait_send()
+        for s in range(nz - 1):
+            @pl.when((z - s >= 0) & (z + 1 < nz))
+            def _():
+                right(t, s).wait_send()
+
+            @pl.when((z + s < nz) & (z >= 1))
+            def _():
+                left(t, s).wait_send()
+
+    gain = gain_ref[...]
+    strip = min(512, rows)
+    tile = min(256, rows)
+    step = half // 3 if half % 384 == 0 else 128
+    blocks = [x, 2 + x, 1 - x, 2 + (1 - x)]
+    own_rows = out_ref.shape[0]
+
+    def norm(t):
+        start = (y if t == 0 else 1 - y) * rows
+
+        @pl.loop(0, rows // 32)
+        def _(p):
+            r = pl.ds(pl.multiple_of(start + p * 32, 32), 32)
+            v = X[r, :].astype(jnp.float32)
+            scale = lax.rsqrt(jnp.mean(v * v, axis=-1, keepdims=True) + 1e-06)
+            X[r, :] = (v * scale * gain).astype(jnp.bfloat16)
+
+    def block_product(block, order):
+        depth = pl.ds(pl.multiple_of(block * rows_w, rows_w), rows_w)
+
+        @pl.loop(0, rows // strip)
+        def _(i):
+            here = pl.ds(pl.multiple_of(i * strip, strip), strip)
+            r = pl.ds(pl.multiple_of((1 - y) * rows + i * strip, strip), strip)
+
+            @pl.loop(0, half // step)
+            def _(j):
+                h = pl.ds(pl.multiple_of(j * step, 128), step)
+                g = jnp.dot(X[r, depth], G[depth, h], preferred_element_type=jnp.float32)
+                u = jnp.dot(X[r, depth], U[depth, h], preferred_element_type=jnp.float32)
+                if order > 0:
+                    g = g + AG[here, h]
+                    u = u + AU[here, h]
+                if order < 3:
+                    AG[here, h] = g
+                    AU[here, h] = u
+                else:
+                    H[r, h] = (g * jax.nn.sigmoid(g) * u).astype(jnp.bfloat16)
+
+    def own_product(low, high):
+        @pl.loop(low, high)
+        def _(i):
+            r = pl.ds(pl.multiple_of(y * rows + i * tile, tile), tile)
+
+            @pl.loop(0, half // step)
+            def _(j):
+                h = pl.ds(pl.multiple_of(j * step, 128), step)
+                g = jnp.dot(X[r, :], G[:, h], preferred_element_type=jnp.float32)
+                u = jnp.dot(X[r, :], U[:, h], preferred_element_type=jnp.float32)
+                H[r, h] = (g * jax.nn.sigmoid(g) * u).astype(jnp.bfloat16)
+
     y_states.start()
     own_states.start()
     wx[0].start()
@@ -155,123 +219,110 @@
     y_states.wait_recv()
     first(1)
     for s in range(nz - 1):
-        relay(0, s)
-        if s == nz - 2:
+        relay(1, s)
+        if s == 0:
             wy[0].wait_recv()
             wr[0].start()
-    for s in range(nz - 1):
-        relay(1, s)
-        if s == 0:
-            wy[1].wait_recv()
-            wr[1].start()
-            wx[2].start()
-    wy[2].wait_recv()
-    wr[2].start()
-    for m in range(3):
-        loc[m].wait()
-    for t in range(2):
-        for zs in range(nz):
-            sib_in(t, zs).wait_recv()
-    for m in range(2):
-        wx[m].wait_recv()
-        wr[m].wait_recv()
-    y_states.wait_send()
-    for t in range(2):
-        for zs in range(nz):
-            sib(t, zs).wait_send()
-        for s in range(nz - 1):
-            @pl.when((z - s >= 0) & (z + 1 < nz))
+    wy[1].wait_recv()
+    wr[1].start()
+    relay(0, 0)
+    settle(1)
+    norm(1)
+    for s in range(1, nz - 1):
+        if s == nz - 2:
+            for m in range(2):
+                loc[m].wait()
+            block_product(b, 0)
+            block_product(by, 1)
+            for m in range(2):
+                wx[m].wait_recv()
+            block_product(bx, 2)
+            wy[2].wait_recv()
+
+            @pl.when(y == 0)
             def _():
-                right(t, s).wait_send()
-
-            @pl.when((z + s < nz) & (z >= 1))
+                wx[2].start()
+                wr[2].start()
+
+            @pl.when(y == 1)
             def _():
-                left(t, s).wait_send()
-
-    tile = N.shape[0]
-    gain = gain_ref[...]
-
-    @pl.loop(0, X.shape[0] // tile)
-    def _(i):
-        r = pl.ds(pl.multiple_of(i * tile, tile), tile)
-
-        @pl.loop(0, tile // 32)
-        def _(p):
-            q = pl.multiple_of(p * 32, 32)
-            v = X[pl.ds(pl.multiple_of(i * tile + q, 32), 32), :].astype(jnp.float32)
-            scale = lax.rsqrt(jnp.mean(v * v, axis=-1, keepdims=True) + 1e-06)
-            N[pl.ds(q, 32), :] = (v * scale * gain).astype(jnp.bfloat16)
-
-        step = half // 3 if (half // 3) % 128 == 0 else 128
-
-        @pl.loop(0, half // step)
-        def _(j):
-            h = pl.ds(pl.multiple_of(j * step, 128), step)
-            g = jnp.dot(N[...], G[:, h], preferred_element_type=jnp.float32)
-            u = jnp.dot(N[...], U[:, h], preferred_element_type=jnp.float32)
-            H[r, h] = (g * jax.nn.sigmoid(g) * u).astype(jnp.bfloat16)
-
-    blocks = [x, 2 + x, 1 - x, 2 + (1 - x)]
-    own_rows = out_ref.shape[0]
+                wr[2].start()
+                wx[2].start()
+
+        relay(0, s)
+    settle(0)
     for j in range(4):
         out_ref[:, pl.ds(pl.multiple_of(blocks[j] * w, w), w)] = X[
             pl.ds(pl.multiple_of(y * rows + z * own_rows, own_rows), own_rows),
             pl.ds(pl.multiple_of(blocks[j] * cols + k * w, w), w),
         ].astype(jnp.float32)
+    norm(0)
+    for m in range(2):
+        wr[m].wait_recv()
+    block_product(bd, 3)
+    loc[2].wait()
 
     base = full // 2
 
     def down_cols(j, core):
         return pl.ds(pl.multiple_of(blocks[j] * cols + core * w, w), w)
 
-    def sib_sum(j):
-        return remote(X.at[:, pl.ds(j * w, w)], SR.at[j], c_sib.at[j], to_sib)
+    def block_rows(t):
+        return pl.ds(pl.multiple_of((y if t == 0 else 1 - y) * rows, rows), rows)
+
+    def sib_sum(t, j):
+        return remote(
+            X.at[block_rows(t), pl.ds(j * w, w)], SR.at[j, block_rows(t), :],
+            c_sib.at[t, j], to_sib,
+        )
 
     def y_sum(j):
-        return remote(X.at[pl.ds(0, rows), pl.ds(base + j * w, w)], YR.at[j], c_y.at[j], to_y)
+        return remote(X.at[block_rows(1), pl.ds(base + j * w, w)], YR.at[j], c_y.at[j], to_y)
 
     def z_sum(j, dz):
         to = lax.rem(z + dz, nz)
         return remote(
             X.at[
-                pl.ds(pl.multiple_of(rows + to * own_rows, own_rows), own_rows),
+                pl.ds(pl.multiple_of(y * rows + to * own_rows, own_rows), own_rows),
                 pl.ds(base + j * w, w),
             ],
             ZR.at[j, dz - 1], c_z.at[j, dz - 1], at_z(to),
         )
 
-    piece = min(512, rows)
-
-    def step_a(j):
-        @pl.loop(0, 2 * rows // piece)
+    def strips(t):
+        start = (y if t == 0 else 1 - y) * rows
+        return lambda i: pl.ds(pl.multiple_of(start + i * strip, strip), strip)
+
+    def step_a(t, j):
+        @pl.loop(0, rows // strip)
         def _(i):
-            r = pl.ds(pl.multiple_of(i * piece, piece), piece)
+            r = strips(t)(i)
             X[r, pl.ds(j * w, w)] = jnp.dot(
                 H[r, :], W[:, down_cols(j, 1 - k)], preferred_element_type=jnp.float32
             ).astype(jnp.bfloat16)
 
-        sib_sum(j).start()
-
-    def step_b(j):
-        sib_sum(j).wait_recv()
-        for put, block in ((0, 1 - y), (1, y)):
-            @pl.loop(0, rows // piece)
-            def _(i):
-                r = pl.ds(pl.multiple_of(block * rows + i * piece, piece), piece)
-                X[pl.ds(pl.multiple_of(put * rows + i * piece, piece), piece), pl.ds(base + j * w, w)] = (
-                    jnp.dot(H[r, :], W[:, down_cols(j, k)], preferred_element_type=jnp.float32)
-                    + SR[j, r, :].astype(jnp.float32)
-                ).astype(jnp.bfloat16)
-
-            if put == 0:
-                y_sum(j).start()
+        sib_sum(t, j).start()
+
+    def step_b(t, j):
+        sib_sum(t, j).wait_recv()
+
+        @pl.loop(0, rows // strip)
+        def _(i):
+            r = strips(t)(i)
+            X[r, pl.ds(base + j * w, w)] = (
+                jnp.dot(H[r, :], W[:, down_cols(j, k)], preferred_element_type=jnp.float32)
+                + SR[j, r, :].astype(jnp.float32)
+            ).astype(jnp.bfloat16)
+
+        if t == 1:
+            y_sum(j).start()
 
     def step_c(j):
         y_sum(j).wait_recv()
 
         @pl.loop(0, rows // own_rows)
         def _(i):
-            r = pl.ds(pl.multiple_of(rows + i * own_rows, own_rows), own_rows)
+            r = pl.ds(pl.multiple_of(y * rows + i * own_rows, own_rows), own_rows)
             here = pl.ds(base + j * w, w)
             X[r, here] = (
                 X[r, here].astype(jnp.float32)
@@ -284,25 +335,45 @@
     def step_e(j):
         here = pl.ds(pl.multiple_of(blocks[j] * w, w), w)
         total = out_ref[:, here] + X[
-            pl.ds(pl.multiple_of(rows + z * own_rows, own_rows), own_rows), pl.ds(base + j * w, w)
+            pl.ds(pl.multiple_of(y * rows + z * own_rows, own_rows), own_rows), pl.ds(base + j * w, w)
         ].astype(jnp.float32)
         for dz in range(1, nz):
             z_sum(j, dz).wait_recv()
             total = total + ZR[j, dz - 1].astype(jnp.float32)
         out_ref[:, here] = total
 
-    step_a(0)
-    step_a(1)
-    step_b(0)
-    step_b(1)
-    wx[2].wait_recv()
-    wr[2].wait_recv()
-    step_a(2)
+    def down_from_x(low):
+        @pl.when(y == (0 if low else 1))
+        def _():
+            wx[2].wait_recv()
+
+        @pl.when(y == (1 if low else 0))
+        def _():
+            wr[2].wait_recv()
+
+    tiles = rows // tile
+    step_a(1, 0)
+    step_a(1, 1)
+    own_product(0, 1)
+    step_b(1, 0)
+    step_b(1, 1)
+    own_product(1, tiles)
+    step_a(0, 0)
+    step_a(0, 1)
+    down_from_x(True)
+    step_a(1, 2)
+    step_a(0, 2)
+    step_b(0, 0)
+    step_b(1, 2)
     step_c(0)
-    step_a(3)
-    step_b(2)
+    step_b(0, 1)
+    step_b(0, 2)
     step_c(1)
-    step_b(3)
+    down_from_x(False)
+    step_a(1, 3)
+    step_a(0, 3)
+    step_b(1, 3)
+    step_b(0, 3)
     step_e(0)
     step_c(2)
     step_e(1)
@@ -310,10 +381,12 @@
     step_e(2)
     step_e(3)
     for j in range(4):
-        sib_sum(j).wait_send()
+        sib_sum(0, j).wait_send()
+        sib_sum(1, j).wait_send()
         y_sum(j).wait_send()
         for dz in range(1, nz):
             z_sum(j, dz).wait_send()
+    y_states.wait_send()
     for m in range(3):
         wx[m].wait_send()
         wy[m].wait_send()
@@ -329,7 +402,6 @@
     w = cols // 2
     own_rows = rows // nz
     dma = pltpu.SemaphoreType.DMA
-    tile = min(512, rows)
     any_spec = pl.BlockSpec(memory_space=pl.ANY)
     vmem = pl.BlockSpec(memory_space=pltpu.VMEM)
     return pl.pallas_call(
@@ -342,14 +414,15 @@
             pltpu.VMEM((full, half), jnp.bfloat16),
             pltpu.VMEM((full, half), jnp.bfloat16),
             pltpu.VMEM((half, full), jnp.bfloat16),
-            pltpu.VMEM((tile, full), jnp.bfloat16),
+            pltpu.VMEM((rows, half), jnp.float32),
+            pltpu.VMEM((rows, half), jnp.float32),
             pltpu.VMEM((2 * rows, half), jnp.bfloat16),
             pltpu.VMEM((4, 2 * rows, w), jnp.bfloat16),
             pltpu.VMEM((4, rows, w), jnp.bfloat16),
             pltpu.VMEM((4, nz - 1, own_rows, w), jnp.bfloat16),
             dma, dma((2,)), dma((2, nz - 1, 2)), dma((2, nz - 1, 2)), dma((2, nz, 2)),
             dma((3,)), dma((3, 2)), dma((3, 2)), dma((3, 2)),
-            dma((4, 2)), dma((4, 2)), dma((4, nz - 1, 2)),
+            dma((2, 4, 2)), dma((4, 2)), dma((4, nz - 1, 2)),
         ],
         compiler_params=pltpu.CompilerParams(
             has_side_effects=True, vmem_limit_bytes=67043328
@@ -472,7 +545,7 @@
             dma, dma((2,)), dma((2,)), dma((devices - 1,)), dma((devices - 1,)),
         ],
         compiler_params=pltpu.CompilerParams(
-            has_side_effects=True, vmem_limit_bytes=40 * 1024 * 1024
+            has_side_effects=True, vmem_limit_bytes=67043328
         ),
     )(resid, gain, hash_weight)
     got = got.reshape(parts, corpus // 2, 2, groups, docs, 128)

time: 365 us -> 311 us (0.85)
  Pallas kernels: 352 us -> 302 us
  local copies, waits for them, and re-layouts: 12.6 us -> 7.85 us
    pallas_call x1, Pallas kernels: 333 us -> 280 us  [wide(): pl.pallas_call(wide_kernel, out_shape=jax.ShapeDtypeStruct((own_rows, ful...]
    unnamed x9 -> x1, local copies, waits for them, and re-layouts: 5.76 us -> 0.09 us
where the time goes in v3:
time: 311 us
  Pallas kernels  302 us (97%)
  local copies, waits for them, and re-layouts  7.85 us (3%)
    pallas_call x1, Pallas kernels, wide(): pl.pallas_call(wide_kernel, out_shape=jax.ShapeDtypeStruct((own_rows, ful...  280 us
    pallas_call x1, Pallas kernels, all_codes(): pl.pallas_call(code_kernel, out_shape=jax.ShapeDtypeStruct((devices, grou...  19.4 us

profile of v3, /device:TPU:0, one launch (start us, length us, event | category | flops | bytes accessed | tf_op | source)
XLA Modules:
  0.0 310.6 jit_solution(17350859893063223032)
XLA Ops:
  0.0 0.7 reshape.14
  0.7 0.6 constant_dynamic-slice_fusion.1
  1.3 280.4 %shard_map.100.resid_ref = f32[256,2048]{1,0:T(8,128)} custom-call(bf16[1024,512]{1,0:T(8,128)(2,1)} %states_ref.1, f32[1,4096]{1,0:T(1,128)} %bitcast.12, bf16[1024,1536]{1,0:T(8,128)(2,1)} %gate_ref.1, bf16[1024,1536]{1,0:T(8,128)(2,1)} %up_ref.1, bf16[1536,1024]{1,0:T(8,128)(2,1)} %down_ref.1), custom_call_target="tpu_custom_call" | custom-call | tf_op jit(solution)/shard_map/pallas_call | solution.py:407
  281.7 19.4 %shard_map.101 = bf16[32,16,128]{2,1,0:T(8,128)(2,1)} custom-call(f32[256,2048]{1,0:T(8,128)} %shard_map.100.resid_ref, f32[1,2048]{1,0:T(1,128)} %bitcast.11, bf16[4096,1024]{1,0:T(8,128)(2,1)} %hash_ref.1), custom_call_target="tpu_custom_call" | custom-call | tf_op jit(solution)/shard_map/pallas_call | solution.py:535
  301.2 1.0 copy.18
  302.1 0.1 reshape.17
  302.2 0.9 convolution_convert_fusion
  303.1 0.7 pad.8.corpus_ref
  303.9 1.7 constant_dynamic-slice_fusion.2.bits_ref
  305.5 0.8 constant_dynamic-slice_fusion
  306.3 0.1 copy.16
  306.4 0.6 pad.9.index_ref
  307.1 2.0 shard_map.102
  309.0 1.6 copy.15

commit v4 on v3

--- a/solution.py
+++ b/solution.py
@@ -6,8 +6,6 @@
 from jax.sharding import PartitionSpec as P
 
 DOC_LEN = 64
-CODE = 1024
-NQ = 4096
 
 
 def rms(values, gain):
@@ -18,25 +16,46 @@
     return jnp.dot(left, piece, preferred_element_type=jnp.float32)
 
 
-def score_kernel(bits_ref, corpus_ref, index_ref, out_ref):
+def score_kernel(place_ref, bits_ref, codes_ref, slot_ref, index_ref, out_ref, picks):
+    docs = codes_ref.shape[0]
+    lanes = picks.shape[1]
+    top = index_ref.shape[1]
+    entry = lax.broadcasted_iota(jnp.int32, (lanes, docs), 0)
+    placing = jnp.where(entry == slot_ref[...], 1.0, 0.0).astype(jnp.bfloat16)
+    corpus = jnp.dot(placing, codes_ref[...], preferred_element_type=jnp.float32).astype(
+        jnp.bfloat16
+    )
     table = lax.dot_general(
         bits_ref[...],
-        corpus_ref[...],
+        corpus,
         (((1,), (1,)), ((), ())),
         preferred_element_type=jnp.float32,
     ) * (1.0 / float(bits_ref.shape[1]) ** 0.5)
-    out_ref[...] = jnp.take_along_axis(table, index_ref[...], axis=1)
-
-
-def score(bits, corpus, index):
-    rows, top = index.shape
-    lanes = 128 * max(pl.cdiv(corpus.shape[0], 128), pl.cdiv(top, 128))
-    corpus = jnp.pad(corpus, ((0, lanes - corpus.shape[0]), (0, 0)))
-    index = jnp.pad(index, ((0, 0), (0, lanes - top)))
-    wide = pl.pallas_call(
-        score_kernel, out_shape=jax.ShapeDtypeStruct((rows, lanes), jnp.float32)
-    )(bits, corpus, index)
-    return wide[:, :top]
+    picks[...] = jnp.zeros_like(picks)
+    picks[:, :top] = index_ref[...]
+    out_ref[...] = jnp.take_along_axis(table, picks[...], axis=1)[:, :top]
+
+
+def score(query_bits, codes, slot_map, query_index, flat_index, rows):
+    docs, bits = codes.shape
+    top = query_index.shape[1]
+    lanes = 128 * max(pl.cdiv(docs, 128), pl.cdiv(top, 128))
+    return pl.pallas_call(
+        score_kernel,
+        out_shape=jax.ShapeDtypeStruct((rows, top), jnp.float32),
+        grid_spec=pltpu.PrefetchScalarGridSpec(
+            num_scalar_prefetch=1,
+            grid=(1,),
+            in_specs=[
+                pl.BlockSpec((rows, bits), lambda i, f: (f[0], 0)),
+                pl.BlockSpec((docs, bits), lambda i, f: (0, 0)),
+                pl.BlockSpec((1, docs), lambda i, f: (0, 0)),
+                pl.BlockSpec((rows, top), lambda i, f: (f[0], 0)),
+            ],
+            out_specs=pl.BlockSpec((rows, top), lambda i, f: (0, 0)),
+            scratch_shapes=[pltpu.VMEM((rows, lanes), jnp.int32)],
+        ),
+    )(flat_index.reshape(1), query_bits, codes, slot_map[None], query_index)
 
 
 def wide_kernel(
@@ -276,17 +295,22 @@
             c_sib.at[t, j], to_sib,
         )
 
-    def y_sum(j):
-        return remote(X.at[block_rows(1), pl.ds(base + j * w, w)], YR.at[j], c_y.at[j], to_y)
-
-    def z_sum(j, dz):
+    hw = w // 2
+
+    def y_sum(j, h):
+        return remote(
+            X.at[block_rows(1), pl.ds(base + j * w + h * hw, hw)],
+            YR.at[j, :, pl.ds(h * hw, hw)], c_y.at[j, h], to_y,
+        )
+
+    def z_sum(j, h, dz):
         to = lax.rem(z + dz, nz)
         return remote(
             X.at[
                 pl.ds(pl.multiple_of(y * rows + to * own_rows, own_rows), own_rows),
-                pl.ds(base + j * w, w),
+                pl.ds(base + j * w + h * hw, hw),
             ],
-            ZR.at[j, dz - 1], c_z.at[j, dz - 1], at_z(to),
+            ZR.at[j, dz - 1, :, pl.ds(h * hw, hw)], c_z.at[j, h, dz - 1], at_z(to),
         )
 
     def strips(t):
@@ -305,42 +329,54 @@
 
     def step_b(t, j):
         sib_sum(t, j).wait_recv()
-
-        @pl.loop(0, rows // strip)
-        def _(i):
-            r = strips(t)(i)
-            X[r, pl.ds(base + j * w, w)] = (
-                jnp.dot(H[r, :], W[:, down_cols(j, k)], preferred_element_type=jnp.float32)
-                + SR[j, r, :].astype(jnp.float32)
-            ).astype(jnp.bfloat16)
-
-        if t == 1:
-            y_sum(j).start()
-
-    def step_c(j):
-        y_sum(j).wait_recv()
+        for h in range(2):
+            down = pl.ds(pl.multiple_of(blocks[j] * cols + k * w + h * hw, hw), hw)
+
+            @pl.loop(0, rows // strip)
+            def _(i):
+                r = strips(t)(i)
+                X[r, pl.ds(base + j * w + h * hw, hw)] = (
+                    jnp.dot(H[r, :], W[:, down], preferred_element_type=jnp.float32)
+                    + SR[j, r, pl.ds(h * hw, hw)].astype(jnp.float32)
+                ).astype(jnp.bfloat16)
+
+            if t == 1:
+                y_sum(j, h).start()
+
+    def half_c(j, h):
+        y_sum(j, h).wait_recv()
 
         @pl.loop(0, rows // own_rows)
         def _(i):
             r = pl.ds(pl.multiple_of(y * rows + i * own_rows, own_rows), own_rows)
-            here = pl.ds(base + j * w, w)
+            here = pl.ds(base + j * w + h * hw, hw)
+            q = pl.ds(pl.multiple_of(i * own_rows, own_rows), own_rows)
             X[r, here] = (
                 X[r, here].astype(jnp.float32)
-                + YR[j, pl.ds(pl.multiple_of(i * own_rows, own_rows), own_rows), :].astype(jnp.float32)
+                + YR[j, q, pl.ds(h * hw, hw)].astype(jnp.float32)
             ).astype(jnp.bfloat16)
 
         for dz in range(1, nz):
-            z_sum(j, dz).start()
-
-    def step_e(j):
-        here = pl.ds(pl.multiple_of(blocks[j] * w, w), w)
+            z_sum(j, h, dz).start()
+
+    def step_c(j):
+        half_c(j, 0)
+        half_c(j, 1)
+
+    def half_e(j, h):
+        here = pl.ds(pl.multiple_of(blocks[j] * w + h * hw, hw), hw)
         total = out_ref[:, here] + X[
-            pl.ds(pl.multiple_of(y * rows + z * own_rows, own_rows), own_rows), pl.ds(base + j * w, w)
+            pl.ds(pl.multiple_of(y * rows + z * own_rows, own_rows), own_rows),
+            pl.ds(base + j * w + h * hw, hw),
         ].astype(jnp.float32)
         for dz in range(1, nz):
-            z_sum(j, dz).wait_recv()
-            total = total + ZR[j, dz - 1].astype(jnp.float32)
+            z_sum(j, h, dz).wait_recv()
+            total = total + ZR[j, dz - 1, :, pl.ds(h * hw, hw)].astype(jnp.float32)
         out_ref[:, here] = total
+
+    def step_e(j):
+        half_e(j, 0)
+        half_e(j, 1)
 
     def down_from_x(low):
         @pl.when(y == (0 if low else 1))
@@ -376,16 +412,18 @@
     step_b(0, 3)
     step_e(0)
     step_c(2)
+    half_c(3, 0)
     step_e(1)
-    step_c(3)
+    half_c(3, 1)
     step_e(2)
     step_e(3)
     for j in range(4):
         sib_sum(0, j).wait_send()
         sib_sum(1, j).wait_send()
-        y_sum(j).wait_send()
-        for dz in range(1, nz):
-            z_sum(j, dz).wait_send()
+        for h in range(2):
+            y_sum(j, h).wait_send()
+            for dz in range(1, nz):
+                z_sum(j, h, dz).wait_send()
     y_states.wait_send()
     for m in range(3):
         wx[m].wait_send()
@@ -422,7 +460,7 @@
             pltpu.VMEM((4, nz - 1, own_rows, w), jnp.bfloat16),
             dma, dma((2,)), dma((2, nz - 1, 2)), dma((2, nz - 1, 2)), dma((2, nz, 2)),
             dma((3,)), dma((3, 2)), dma((3, 2)), dma((3, 2)),
-            dma((2, 4, 2)), dma((4, 2)), dma((4, nz - 1, 2)),
+            dma((2, 4, 2)), dma((4, 2, 2)), dma((4, 2, nz - 1, 2)),
         ],
         compiler_params=pltpu.CompilerParams(
             has_side_effects=True, vmem_limit_bytes=67043328
@@ -606,17 +644,8 @@
         gathered = all_codes(wide(*layer), final_gain, hash_weight)
     else:
         gathered = plain_codes(*layer, final_gain, hash_weight)
-    doc_total = gathered.shape[0]
-    placing = (slot_map[:, None] == jnp.arange(doc_total, dtype=jnp.int32)[None, :]).astype(
-        jnp.bfloat16
-    )
-    corpus = jnp.einsum("ds,dc->sc", placing, gathered, preferred_element_type=jnp.float32).astype(
-        jnp.bfloat16
-    )
-    query_rows = NQ // devices
-    my_bits = lax.dynamic_slice_in_dim(query_bits, flat_index * query_rows, query_rows, 0)
-    my_index = lax.dynamic_slice_in_dim(query_index, flat_index * query_rows, query_rows, 0)
-    return score(my_bits, corpus, my_index)
+    query_rows = query_bits.shape[0] // devices
+    return score(query_bits, gathered, slot_map, query_index, flat_index, query_rows)
 
 
 def solution(mesh):

time: 311 us -> 309 us (level)
  no operation moved by 1% of the time
where the time goes in v4:
time: 309 us
  Pallas kernels  302 us (98%)
  local copies, waits for them, and re-layouts  7.49 us (2%)
    pallas_call x1, Pallas kernels, wide(): pl.pallas_call(wide_kernel, out_shape=jax.ShapeDtypeStruct((own_rows, ful...  279 us
    pallas_call x1, Pallas kernels, all_codes(): pl.pallas_call(code_kernel, out_shape=jax.ShapeDtypeStruct((devices, grou...  20 us

profile of v4, /device:TPU:0, one launch (start us, length us, event | category | flops | bytes accessed | tf_op | source)
XLA Modules:
  0.0 309.1 jit_solution(10426110731646490322)
XLA Ops:
  0.0 0.7 reshape.17
  0.7 0.6 constant_dynamic-slice_fusion
  1.3 279.3 %shard_map.100.resid_ref = f32[256,2048]{1,0:T(8,128)} custom-call(bf16[1024,512]{1,0:T(8,128)(2,1)} %states_ref.1, f32[1,4096]{1,0:T(1,128)} %bitcast.11, bf16[1024,1536]{1,0:T(8,128)(2,1)} %gate_ref.1, bf16[1024,1536]{1,0:T(8,128)(2,1)} %up_ref.1, bf16[1536,1024]{1,0:T(8,128)(2,1)} %down_ref.1), custom_call_target="tpu_custom_call" | custom-call | tf_op jit(solution)/shard_map/pallas_call | solution.py:445
  280.7 20.0 %shard_map.101 = bf16[32,16,128]{2,1,0:T(8,128)(2,1)} custom-call(f32[256,2048]{1,0:T(8,128)} %shard_map.100.resid_ref, f32[1,2048]{1,0:T(1,128)} %bitcast.10, bf16[4096,1024]{1,0:T(8,128)(2,1)} %hash_ref.1), custom_call_target="tpu_custom_call" | custom-call | tf_op jit(solution)/shard_map/pallas_call | solution.py:573
  300.7 1.0 copy.18
  301.7 0.7 reshape.20.codes_ref
  302.4 2.9 copy.15.index_ref
  305.3 2.2 shard_map.102
  307.5 1.6 copy.16

commit v5 on v4

--- a/solution.py
+++ b/solution.py
@@ -40,6 +40,7 @@
     docs, bits = codes.shape
     top = query_index.shape[1]
     lanes = 128 * max(pl.cdiv(docs, 128), pl.cdiv(top, 128))
+    query_index = lax.dynamic_slice_in_dim(query_index, flat_index * rows, rows, 0)
     return pl.pallas_call(
         score_kernel,
         out_shape=jax.ShapeDtypeStruct((rows, top), jnp.float32),
@@ -50,7 +51,7 @@
                 pl.BlockSpec((rows, bits), lambda i, f: (f[0], 0)),
                 pl.BlockSpec((docs, bits), lambda i, f: (0, 0)),
                 pl.BlockSpec((1, docs), lambda i, f: (0, 0)),
-                pl.BlockSpec((rows, top), lambda i, f: (f[0], 0)),
+                pl.BlockSpec((rows, top), lambda i, f: (0, 0)),
             ],
             out_specs=pl.BlockSpec((rows, top), lambda i, f: (0, 0)),
             scratch_shapes=[pltpu.VMEM((rows, lanes), jnp.int32)],

time: 309 us -> 308 us (level)
  no operation moved by 1% of the time
where the time goes in v5:
time: 308 us
  Pallas kernels  302 us (98%)
  local copies, waits for them, and re-layouts  6.1 us (2%)
    pallas_call x1, Pallas kernels, wide(): pl.pallas_call(wide_kernel, out_shape=jax.ShapeDtypeStruct((own_rows, ful...  279 us
    pallas_call x1, Pallas kernels, all_codes(): pl.pallas_call(code_kernel, out_shape=jax.ShapeDtypeStruct((devices, grou...  20 us

profile of v5, /device:TPU:0, one launch (start us, length us, event | category | flops | bytes accessed | tf_op | source)
XLA Modules:
  0.0 307.7 jit_solution(5601858338716268341)
XLA Ops:
  0.0 279.3 %shard_map.100.resid_ref = f32[256,2048]{1,0:T(8,128)} custom-call(bf16[1024,512]{1,0:T(8,128)(2,1)} %states_ref.1, f32[1,4096]{1,0:T(1,128)} %bitcast.11, bf16[1024,1536]{1,0:T(8,128)(2,1)} %gate_ref.1, bf16[1024,1536]{1,0:T(8,128)(2,1)} %up_ref.1, bf16[1536,1024]{1,0:T(8,128)(2,1)} %down_ref.1), custom_call_target="tpu_custom_call" | custom-call | tf_op jit(solution)/shard_map/pallas_call | solution.py:446
  279.4 0.7 reshape.17
  280.1 0.6 constant_dynamic-slice_fusion.1
  280.7 20.0 %shard_map.101 = bf16[32,16,128]{2,1,0:T(8,128)(2,1)} custom-call(f32[256,2048]{1,0:T(8,128)} %shard_map.100.resid_ref, f32[1,2048]{1,0:T(1,128)} %bitcast.10, bf16[4096,1024]{1,0:T(8,128)(2,1)} %hash_ref.1), custom_call_target="tpu_custom_call" | custom-call | tf_op jit(solution)/shard_map/pallas_call | solution.py:574
  300.7 1.0 copy.19
  301.7 0.7 reshape.20.codes_ref
  302.4 0.8 constant_dynamic-slice_fusion
  303.2 0.7 copy.17.index_ref
  303.9 2.2 shard_map.102
  306.1 1.6 copy.16
